TPU v7x, 256 devices: a whole 4x4x8 slice. The times are simulated.
256 devices in a mesh: section: 2 (over core), blk: 128 (over z, x, y).
Axes of the slice: x: 4, y: 4, z: 8, core: 2. Of those that a mesh axis runs over, the one named last changes fastest.
Arguments:
- hidden: bfloat16 [2, 384, 3072], P(None, 'blk'), may hold values from -4 to 4
- qkv_weight: bfloat16 [2, 3072, 9216], P('section', None, 'blk'), may hold values from -0.109375 to 0.109375
- out_weight: bfloat16 [2, 3072, 3072], P('section', None, 'blk'), may hold values from -0.109375 to 0.109375
- modulation: float32 [2, 50, 3, 3072], P('section'), may hold values from -3 to 3
- timestep: int32 [1], replicated, may hold values from 0 to 49
- fresh: int32 [2, 2, 128], P('section'), may hold values 0 or 1
- live: int32 [2, 128], replicated, may hold values from 0 to 1, as said below
- k_stale: bfloat16 [2, 2, 384, 3072], P('section', None, 'blk'), may hold values from -6 to 6
- v_stale: bfloat16 [2, 2, 384, 3072], P('section', None, 'blk'), may hold values from -16 to 16
Outputs:
- layer_outputs: bfloat16 [2, 2, 384, 3072], P('section', None, 'blk')
Inputs may be any that keep to these rules, and one draw needn't show every extreme that they name: Block 0 of every request is live.
All inputs are finite; a program needn't handle non-finite values. No bound on the sum of `fresh` on one device may be relied on, other than what follows from the above.
Results may differ from a plain program's by a relative error of at most 0.017.
Values may be sent and summed in bfloat16 or wider, within the bound.
A program may use at most 64 MiB of HBM per device.

v0:
```python
import jax
import jax.numpy as jnp
from jax import lax
from jax.sharding import PartitionSpec as P


def from_behind(shard, axis, by):
    count = lax.axis_size(axis)
    pairs = [(i, i + by) for i in range(count) if 0 <= i + by < count]
    return lax.ppermute(shard, axis, pairs)


def attend(layer_in, qkv_cols, out_cols, modulate, fresh_own, old_keys, old_values, live):
    stream = layer_in.astype(jnp.float32)
    center = jnp.mean(stream, axis=-1, keepdims=True)
    variance = jnp.mean((stream - center) ** 2, axis=-1, keepdims=True)
    normed = (stream - center) / jnp.sqrt(variance + 1e-06) * (1.0 + modulate[0]) + modulate[1]
    normed_b = normed.astype(jnp.bfloat16)
    columns = jnp.einsum(
        "rnd,dc->rnc",
        lax.all_gather(normed_b, "blk", axis=1, tiled=True),
        qkv_cols,
        preferred_element_type=jnp.float32,
    ).astype(jnp.bfloat16)
    projected = lax.all_to_all(columns, "blk", split_axis=1, concat_axis=2, tiled=True)
    num_req, num_rows, width = layer_in.shape
    queries = projected[:, :, :width]
    new_keys = projected[:, :, width : 2 * width]
    new_values = projected[:, :, 2 * width :]
    use_fresh = (fresh_own == 1)[:, None, None]
    keys = jnp.where(use_fresh, new_keys, old_keys)
    values = jnp.where(use_fresh, new_values, old_values)
    num_heads = width // 64
    num_blocks = live.shape[1]
    q_heads = queries.reshape(num_req, num_rows, num_heads, 64)
    live_float = live.astype(jnp.float32)
    run_max = jnp.full((num_req, num_heads, num_rows), -1e30, jnp.float32)
    key_piece = lax.all_gather(keys, "blk", axis=1, tiled=True)
    value_piece = lax.all_gather(values, "blk", axis=1, tiled=True)
    piece_rows = key_piece.shape[1]
    key_heads = key_piece.reshape(num_req, piece_rows, num_heads, 64)
    value_heads = value_piece.reshape(num_req, piece_rows, num_heads, 64)
    scores = (
        jnp.einsum("qrhd,qnhd->qhrn", q_heads, key_heads, preferred_element_type=jnp.float32)
        * 0.125
    )
    block_ids = jnp.arange(piece_rows) // num_rows
    one_hot = (block_ids[:, None] == jnp.arange(num_blocks)[None, :]).astype(jnp.float32)
    usable = jnp.einsum("qb,nb->qn", live_float, one_hot) > 0.5
    usable = usable[:, None, None, :]
    scores = jnp.where(usable, scores, -1e30)
    new_max = jnp.maximum(run_max, jnp.max(scores, axis=-1))
    weights = jnp.where(usable, jnp.exp(scores - new_max[..., None]), 0.0)
    new_sum = jnp.sum(weights, axis=-1)
    new_acc = jnp.einsum(
        "qhrn,qnhd->qhrd", weights, value_heads.astype(jnp.float32), precision=lax.Precision.HIGHEST
    )
    attn = new_acc / new_sum[..., None]
    attn = jnp.transpose(attn, (0, 2, 1, 3)).reshape(num_req, num_rows, width).astype(jnp.bfloat16)
    out_part = jnp.einsum(
        "rnd,dc->rnc",
        lax.all_gather(attn, "blk", axis=1, tiled=True),
        out_cols,
        preferred_element_type=jnp.float32,
    ).astype(jnp.bfloat16)
    mixed_back = lax.all_to_all(out_part, "blk", split_axis=1, concat_axis=2, tiled=True)
    return (stream + modulate[2] * mixed_back.astype(jnp.float32)).astype(jnp.bfloat16)


def pick_request(array, req_idx):
    return lax.dynamic_index_in_dim(array, req_idx, 0, keepdims=True)


def per_device(hidden, qkv_weight, out_weight, modulation, timestep, fresh, live, k_stale, v_stale):
    section_idx = lax.axis_index("section")
    block_idx = lax.axis_index("blk")
    steps_all = modulation.shape[1]
    pick_row = (jnp.arange(steps_all) == timestep[0]).astype(jnp.float32)
    modulate = jnp.einsum("t,tcd->cd", pick_row, modulation[0], precision=lax.Precision.HIGHEST)
    num_blocks = fresh.shape[2]
    own_column = (jnp.arange(num_blocks) == block_idx).astype(jnp.int32)
    fresh_own = jnp.sum(fresh[0] * own_column[None, :], axis=1)
    qkv_cols = qkv_weight[0]
    out_cols = out_weight[0]
    old_keys = k_stale[0]
    old_values = v_stale[0]
    num_req = hidden.shape[0]
    received = jnp.zeros_like(hidden[0:1])
    first_out = []
    second_out = []
    for tick_idx in range(num_req + 1):
        if tick_idx < num_req:
            own_input = hidden[tick_idx : tick_idx + 1]
        else:
            own_input = jnp.zeros_like(hidden[0:1])
        layer_in = jnp.where(section_idx == 0, own_input, received)
        req_idx = jnp.clip(tick_idx - section_idx, 0, num_req - 1)
        layer_out = attend(
            layer_in,
            qkv_cols,
            out_cols,
            modulate,
            pick_request(fresh_own, req_idx),
            pick_request(old_keys, req_idx),
            pick_request(old_values, req_idx),
            pick_request(live, req_idx),
        )
        if tick_idx < num_req:
            first_out.append(layer_out)
            received = from_behind(layer_out, "section", 1)
        if tick_idx >= 1:
            second_out.append(layer_out)
    result = jnp.where(
        section_idx == 0, jnp.concatenate(first_out, axis=0), jnp.concatenate(second_out, axis=0)
    )
    return result[None]


def solution(mesh):
    return jax.shard_map(
        per_device,
        mesh=mesh,
        in_specs=(
            P(None, "blk", None),
            P("section", None, "blk"),
            P("section", None, "blk"),
            P("section", None, None, None),
            P(),
            P("section", None, None),
            P(),
            P("section", None, "blk", None),
            P("section", None, "blk", None),
        ),
        out_specs=P("section", None, "blk", None),
        check_vma=False,
    )
```

profile of v0, /device:TPU:2, one launch (start us, length us, event | category | flops | bytes accessed | tf_op | source)
XLA Modules:
  0.0 1597.2 jit_solution(17317601868942555664)
XLA Ops:
  6.6 1.0 fusion.114
  7.6 1.0 multiply_reduce_fusion.2
  9.2 2.4 fusion.18
  12.8 120.3 %all-gather.13.cloned.1.call-done = bf16[1,384,3072]{2,0,1:T(2,128)(2,1)} async-done(((bf16[1,3,3072]{2,0,1:T(2,128)(2,1)}), bf16[1,384,3072]{2,0,1:T(2,128)(2,1)}) %all-gather.13.cloned.1.call-update) | async-done | bytes 2359312 | tf_op jit(solution)/shard_map/all_gather | solution.py:21
  133.0 3.2 fusion.42
  136.3 0.8 copy.110
  137.1 9.1 all-to-all-start
  147.7 11.1 all-to-all-done
  161.5 109.9 %all-gather.15.cloned.1.call-done = bf16[1,384,3072]{2,0,1:T(2,128)(2,1)} async-done(((bf16[1,3,3072]{2,0,1:T(2,128)(2,1)}), bf16[1,384,3072]{2,0,1:T(2,128)(2,1)}) %all-gather.15.cloned.1.call-update) | async-done | bytes 2359312 | tf_op jit(solution)/shard_map/all_gather | solution.py:38
  271.4 10.0 copy.113
  282.3 107.0 %all-gather.17.cloned.1.call-done = bf16[1,384,3072]{2,0,1:T(2,128)(2,1)} async-done(((bf16[1,3,3072]{2,0,1:T(2,128)(2,1)}), bf16[1,384,3072]{2,0,1:T(2,128)(2,1)}) %all-gather.17.cloned.1.call-update) | async-done | bytes 2359312 | tf_op jit(solution)/shard_map/all_gather | solution.py:39
  389.2 10.0 copy.116
  399.2 2.6 fusion.47
  402.6 114.2 %all-gather.19.cloned.1.call-done = bf16[1,384,3072]{2,0,1:T(2,128)(2,1)} async-done(((bf16[1,3,3072]{2,0,1:T(2,128)(2,1)}), bf16[1,384,3072]{2,0,1:T(2,128)(2,1)}) %all-gather.19.cloned.1.call-update) | async-done | bytes 2359312 | tf_op jit(solution)/shard_map/all_gather | solution.py:62
  516.8 3.1 fusion.63
  520.1 21.4 %all_to_all.81 = bf16[1,384,24]{2,0,1:T(2,128)(2,1)S(1)} all-to-all(bf16[1,384,24]{2,0,1:T(2,128)(2,1)S(1)} %copy.119), channel_id=1, replica_groups=mesh['section'=2,'blk'=128] {'blk'}, dimensions={1} | all-to-all | bytes 36864 | tf_op jit(solution)/shard_map/all_to_all | solution.py:66
  542.0 1.3 collective-permute-start
  543.3 0.8 collective-permute-done
  545.3 111.1 %all-gather.21.cloned.1.call-done = bf16[1,384,3072]{2,0,1:T(2,128)(2,1)} async-done(((bf16[1,3,3072]{2,0,1:T(2,128)(2,1)}), bf16[1,384,3072]{2,0,1:T(2,128)(2,1)}) %all-gather.21.cloned.1.call-update) | async-done | bytes 2359312 | tf_op jit(solution)/shard_map/all_gather | solution.py:21
  656.5 3.2 fusion.39
  659.7 0.8 copy.121
  660.5 9.1 all-to-all-start.2
  670.2 11.9 all-to-all-done.2
  684.9 109.9 %all-gather.23.cloned.1.call-done = bf16[1,384,3072]{2,0,1:T(2,128)(2,1)} async-done(((bf16[1,3,3072]{2,0,1:T(2,128)(2,1)}), bf16[1,384,3072]{2,0,1:T(2,128)(2,1)}) %all-gather.23.cloned.1.call-update) | async-done | bytes 2359312 | tf_op jit(solution)/shard_map/all_gather | solution.py:38
  794.9 10.0 copy.124
  805.7 106.9 %all-gather.25.cloned.1.call-done = bf16[1,384,3072]{2,0,1:T(2,128)(2,1)} async-done(((bf16[1,3,3072]{2,0,1:T(2,128)(2,1)}), bf16[1,384,3072]{2,0,1:T(2,128)(2,1)}) %all-gather.25.cloned.1.call-update) | async-done | bytes 2359312 | tf_op jit(solution)/shard_map/all_gather | solution.py:39
  912.6 10.0 copy.127
  922.6 2.6 fusion.46
  926.0 114.2 %all-gather.27.cloned.1.call-done = bf16[1,384,3072]{2,0,1:T(2,128)(2,1)} async-done(((bf16[1,3,3072]{2,0,1:T(2,128)(2,1)}), bf16[1,384,3072]{2,0,1:T(2,128)(2,1)}) %all-gather.27.cloned.1.call-update) | async-done | bytes 2359312 | tf_op jit(solution)/shard_map/all_gather | solution.py:62
  1040.2 3.1 fusion.60
  1043.5 21.4 %all_to_all.82 = bf16[1,384,24]{2,0,1:T(2,128)(2,1)S(1)} all-to-all(bf16[1,384,24]{2,0,1:T(2,128)(2,1)S(1)} %copy.130), channel_id=1, replica_groups=mesh['section'=2,'blk'=128] {'blk'}, dimensions={1} | all-to-all | bytes 36864 | tf_op jit(solution)/shard_map/all_to_all | solution.py:66
  1065.4 1.5 collective-permute-start.1
  1067.9 0.7 add_convert_fusion.1
  1068.7 111.1 %all-gather.29.cloned.1.call-done = bf16[1,384,3072]{2,0,1:T(2,128)(2,1)} async-done(((bf16[1,3,3072]{2,0,1:T(2,128)(2,1)}), bf16[1,384,3072]{2,0,1:T(2,128)(2,1)}) %all-gather.29.cloned.1.call-update) | async-done | bytes 2359312 | tf_op jit(solution)/shard_map/all_gather | solution.py:21
  1179.8 3.2 fusion.36
  1183.0 0.8 copy.132
  1183.9 9.1 all-to-all-start.4
  1193.6 11.9 all-to-all-done.4
  1208.2 109.9 %all-gather.31.cloned.1.call-done = bf16[1,384,3072]{2,0,1:T(2,128)(2,1)} async-done(((bf16[1,3,3072]{2,0,1:T(2,128)(2,1)}), bf16[1,384,3072]{2,0,1:T(2,128)(2,1)}) %all-gather.31.cloned.1.call-update) | async-done | bytes 2359312 | tf_op jit(solution)/shard_map/all_gather | solution.py:38
  1318.2 10.0 copy.135
  1329.0 107.0 %all-gather.33.cloned.1.call-done = bf16[1,384,3072]{2,0,1:T(2,128)(2,1)} async-done(((bf16[1,3,3072]{2,0,1:T(2,128)(2,1)}), bf16[1,384,3072]{2,0,1:T(2,128)(2,1)}) %all-gather.33.cloned.1.call-update) | async-done | bytes 2359312 | tf_op jit(solution)/shard_map/all_gather | solution.py:39
  1436.0 10.0 copy.138
  1445.9 2.6 fusion.45
  1449.3 114.2 %all-gather.35.cloned.1.call-done = bf16[1,384,3072]{2,0,1:T(2,128)(2,1)} async-done(((bf16[1,3,3072]{2,0,1:T(2,128)(2,1)}), bf16[1,384,3072]{2,0,1:T(2,128)(2,1)}) %all-gather.35.cloned.1.call-update) | async-done | bytes 2359312 | tf_op jit(solution)/shard_map/all_gather | solution.py:62
  1563.5 3.1 fusion.57
  1566.7 0.9 copy.141
  1567.5 9.1 all-to-all-start.5
  1576.6 12.5 all-to-all-done.5
  (122 shorter events, 19.5 us)
Async XLA Ops:
  6.5 126.5 %copy-start = (bf16[1,3072,72]{1,2,0:T(8,128)(2,1)S(1)}, bf16[1,3072,72]{1,2,0:T(8,128)(2,1)}, u32[]{:S(2)}) copy-start(bf16[1,3072,72]{1,2,0:T(8,128)(2,1)} %param.10) | copy-start | bytes 1327108
  6.5 5.1 copy-start.1
  6.5 6.0 copy-start.3
  6.5 6.0 copy-start.2
  6.5 126.5 %all-gather.13.cloned.1.call-start = ((), (), s32[]{:S(2)}) async-start(), calls=%async_computation.6 | async-start | bytes 4755456 | tf_op jit(solution)/shard_map/all_gather | solution.py:21
  12.5 133.8 %copy-start.4 = (s32[1,2,128]{2,1,0:T(2,128)S(1)}, s32[1,2,128]{2,1,0:T(2,128)}, u32[]{:S(2)}) copy-start(s32[1,2,128]{2,1,0:T(2,128)} %param.14) | copy-start | bytes 3076
  12.8 148.4 %copy-start.6 = (s32[2,128]{1,0:T(2,128)S(1)}, s32[2,128]{1,0:T(2,128)}, u32[]{:S(2)}) copy-start(s32[2,128]{1,0:T(2,128)} %param.15) | copy-start | bytes 3076
  137.1 21.6 %all-to-all-start = ((bf16[1,384,72]{2,0,1:T(2,128)(2,1)}), bf16[1,384,72]{2,0,1:T(2,128)(2,1)S(1)}, u32[]{:S(2)}, u32[]{:S(2)}) async-start(bf16[1,384,72]{2,0,1:T(2,128)(2,1)} %copy.110), calls=%async_computation | async-start | bytes 393216 | tf_op jit(solution)/shard_map/all_to_all | solution.py:25
  146.2 125.2 %all-gather.15.cloned.1.call-start = ((), (), s32[]{:S(2)}) async-start(), calls=%async_computation.7 | async-start | bytes 4755456 | tf_op jit(solution)/shard_map/all_gather | solution.py:38
  160.4 228.9 %all-gather.17.cloned.1.call-start = ((), (), s32[]{:S(2)}) async-start(), calls=%async_computation.8 | async-start | bytes 4755456 | tf_op jit(solution)/shard_map/all_gather | solution.py:39
  161.1 355.7 %all-gather.19.cloned.1.call-start = ((), (), s32[]{:S(2)}) async-start(), calls=%async_computation.9 | async-start | bytes 4755456 | tf_op jit(solution)/shard_map/all_gather | solution.py:62
  399.2 117.6 %copy-start.5 = (bf16[1,3072,24]{1,2,0:T(8,128)(2,1)S(1)}, bf16[1,3072,24]{1,2,0:T(8,128)(2,1)}, u32[]{:S(2)}) copy-start(bf16[1,3072,24]{1,2,0:T(8,128)(2,1)} %param.11) | copy-start | bytes 442372
  402.6 253.9 %all-gather.21.cloned.1.call-start = ((), (), s32[]{:S(2)}) async-start(), calls=%async_computation.10 | async-start | bytes 4755456 | tf_op jit(solution)/shard_map/all_gather | solution.py:21
  542.0 2.1 collective-permute-start
  660.5 21.6 %all-to-all-start.2 = ((bf16[1,384,72]{2,0,1:T(2,128)(2,1)}), bf16[1,384,72]{2,0,1:T(2,128)(2,1)S(1)}, u32[]{:S(2)}, u32[]{:S(2)}) async-start(bf16[1,384,72]{2,0,1:T(2,128)(2,1)} %copy.121), calls=%async_computation.2 | async-start | bytes 393216 | tf_op jit(solution)/shard_map/all_to_all | solution.py:25
  669.6 125.2 %all-gather.23.cloned.1.call-start = ((), (), s32[]{:S(2)}) async-start(), calls=%async_computation.11 | async-start | bytes 4755456 | tf_op jit(solution)/shard_map/all_gather | solution.py:38
  683.8 228.9 %all-gather.25.cloned.1.call-start = ((), (), s32[]{:S(2)}) async-start(), calls=%async_computation.12 | async-start | bytes 4755456 | tf_op jit(solution)/shard_map/all_gather | solution.py:39
  684.5 355.7 %all-gather.27.cloned.1.call-start = ((), (), s32[]{:S(2)}) async-start(), calls=%async_computation.13 | async-start | bytes 4755456 | tf_op jit(solution)/shard_map/all_gather | solution.py:62
  926.0 253.8 %all-gather.29.cloned.1.call-start = ((), (), s32[]{:S(2)}) async-start(), calls=%async_computation.14 | async-start | bytes 4755456 | tf_op jit(solution)/shard_map/all_gather | solution.py:21
  1065.4 2.1 collective-permute-start.1
  1183.9 21.6 %all-to-all-start.4 = ((bf16[1,384,72]{2,0,1:T(2,128)(2,1)}), bf16[1,384,72]{2,0,1:T(2,128)(2,1)S(1)}, u32[]{:S(2)}, u32[]{:S(2)}) async-start(bf16[1,384,72]{2,0,1:T(2,128)(2,1)} %copy.132), calls=%async_computation.4 | async-start | bytes 393216 | tf_op jit(solution)/shard_map/all_to_all | solution.py:25
  1193.0 125.2 %all-gather.31.cloned.1.call-start = ((), (), s32[]{:S(2)}) async-start(), calls=%async_computation.15 | async-start | bytes 4755456 | tf_op jit(solution)/shard_map/all_gather | solution.py:38
  1207.1 228.9 %all-gather.33.cloned.1.call-start = ((), (), s32[]{:S(2)}) async-start(), calls=%async_computation.16 | async-start | bytes 4755456 | tf_op jit(solution)/shard_map/all_gather | solution.py:39
  1207.8 355.7 %all-gather.35.cloned.1.call-start = ((), (), s32[]{:S(2)}) async-start(), calls=%async_computation.17 | async-start | bytes 4755456 | tf_op jit(solution)/shard_map/all_gather | solution.py:62
  1567.5 21.6 %all-to-all-start.5 = ((bf16[1,384,24]{2,0,1:T(2,128)(2,1)}), bf16[1,384,24]{2,0,1:T(2,128)(2,1)S(1)}, u32[]{:S(2)}, u32[]{:S(2)}) async-start(bf16[1,384,24]{2,0,1:T(2,128)(2,1)} %copy.141), calls=%async_computation.5 | async-start | bytes 393216 | tf_op jit(solution)/shard_map/all_to_all | solution.py:66
Sparse Core Ops, SparseCore 0:
  12.6 120.4 all-gather.12
  160.5 110.9 all-gather.14
  275.1 114.0 all-gather.16
  402.7 114.0 all-gather.18
  545.4 110.9 all-gather.20
  683.9 110.9 all-gather.22
  798.5 114.0 all-gather.24
  926.1 114.0 all-gather.26
  1068.8 110.9 all-gather.28
  1207.2 110.9 all-gather.30
  1321.9 114.0 all-gather.32
  1449.4 114.0 all-gather.34
where the time goes:
time: 1600 us
  waiting for transfers between devices  1380 us (86%)
  local copies, waits for them, and re-layouts  72.8 us (5%)
  blocking collectives  42.8 us (3%)
  starting transfers between devices  39.6 us (2%)
  matrix products  31.9 us (2%)
  between operations  16.6 us (1%)
    all_gather x3, waiting for transfers between devices, attend(): lax.all_gather(attn, 'blk', axis=1, tiled=True)  343 us
    all_gather x3, waiting for transfers between devices, attend(): lax.all_gather(normed_b, 'blk', axis=1, tiled=True)  343 us
    all_gather x3, waiting for transfers between devices, attend(): key_piece = lax.all_gather(keys, 'blk', axis=1, tiled=True)  330 us
    all_gather x3, waiting for transfers between devices, attend(): value_piece = lax.all_gather(values, 'blk', axis=1, tiled=True)  321 us
    all_to_all x2, blocking collectives, attend(): lax.all_to_all(out_part, 'blk', split_axis=1, concat_axis=2, tiled=True)  42.8 us
    all_to_all x3, waiting for transfers between devices, attend(): lax.all_to_all(columns, 'blk', split_axis=1, concat_axis=2, tiled=True)  34.9 us
  transfers between devices with their start and end apart: 18, of which 18 were waited for; matrix products, arithmetic and copies ran while one was open for 2% of the time, Pallas kernels for 0%

commit v1 on v0

--- a/solution.py
+++ b/solution.py
@@ -35,8 +35,11 @@
     q_heads = queries.reshape(num_req, num_rows, num_heads, 64)
     live_float = live.astype(jnp.float32)
     run_max = jnp.full((num_req, num_heads, num_rows), -1e30, jnp.float32)
-    key_piece = lax.all_gather(keys, "blk", axis=1, tiled=True)
-    value_piece = lax.all_gather(values, "blk", axis=1, tiled=True)
+    key_piece, value_piece = jnp.split(
+        lax.all_gather(jnp.concatenate([keys, values], axis=0), "blk", axis=1, tiled=True),
+        [keys.shape[0]],
+        axis=0,
+    )
     piece_rows = key_piece.shape[1]
     key_heads = key_piece.reshape(num_req, piece_rows, num_heads, 64)
     value_heads = value_piece.reshape(num_req, piece_rows, num_heads, 64)

time: 1600 us -> 1320 us (0.82)
  waiting for transfers between devices: 1380 us -> 1070 us
  local copies, waits for them, and re-layouts: 72.8 us -> 103 us
    all_gather x6 -> x3, waiting for transfers between devices: 651 us -> 332 us  [attend(): lax.all_gather(jnp.concatenate([keys, values], axis=0), 'blk', axis=1, ti...]
    split x0 -> x9, local copies, waits for them, and re-layouts: none -> 92.2 us  [attend(): jnp.split(lax.all_gather(jnp.concatenate([keys, values], axis=0), 'blk',...]
    all_gather x6 -> x0, local copies, waits for them, and re-layouts: 59.8 us -> none  [the longest x3 29.9 us: attend(): key_piece = lax.all_gather(keys, 'blk', axis=1, tiled=True)]
  transfers between devices with their start and end apart: 18 -> 15, of which waited for: 18 -> 15; matrix products, arithmetic and copies ran while one was open for 2% -> 0% of each run, Pallas kernels for 0% -> 0%
where the time goes in v1:
time: 1320 us; the launch traced here: 1310 us
  waiting for transfers between devices  1070 us (81%)
  local copies, waits for them, and re-layouts  103 us (8%)
  blocking collectives  42.8 us (3%)
  starting transfers between devices  39.3 us (3%)
  matrix products  31.9 us (2%)
  between operations  16.6 us (1%)
    all_gather x3, waiting for transfers between devices, attend(): lax.all_gather(attn, 'blk', axis=1, tiled=True)  343 us
    all_gather x3, waiting for transfers between devices, attend(): lax.all_gather(normed_b, 'blk', axis=1, tiled=True)  343 us
    all_gather x3, waiting for transfers between devices, attend(): lax.all_gather(jnp.concatenate([keys, values], axis=0), 'blk', axis=1, ti...  332 us
    split x9, local copies, waits for them, and re-layouts, attend(): jnp.split(lax.all_gather(jnp.concatenate([keys, values], axis=0), 'blk',...  92.2 us
    all_to_all x2, blocking collectives, attend(): lax.all_to_all(out_part, 'blk', split_axis=1, concat_axis=2, tiled=True)  42.8 us
    all_to_all x3, waiting for transfers between devices, attend(): lax.all_to_all(columns, 'blk', split_axis=1, concat_axis=2, tiled=True)  34.8 us
    all_to_all x3, starting transfers between devices, attend(): lax.all_to_all(columns, 'blk', split_axis=1, concat_axis=2, tiled=True)  27.2 us
  transfers between devices with their start and end apart: 15, of which 15 were waited for; matrix products, arithmetic and copies ran while one was open for 0% of the time, Pallas kernels for 0%

profile of v1, /device:TPU:2, one launch (start us, length us, event | category | flops | bytes accessed | tf_op | source)
XLA Modules:
  0.0 1309.0 jit_solution(4533474868222683579)
XLA Ops:
  6.6 1.0 fusion.114
  7.6 1.0 multiply_reduce_fusion.2
  9.2 2.4 fusion.18
  12.8 120.3 %all-gather.10.cloned.1.call-done = bf16[1,384,3072]{2,0,1:T(2,128)(2,1)} async-done(((bf16[1,3,3072]{2,0,1:T(2,128)(2,1)}), bf16[1,384,3072]{2,0,1:T(2,128)(2,1)}) %all-gather.10.cloned.1.call-update) | async-done | bytes 2359312 | tf_op jit(solution)/shard_map/all_gather | solution.py:21
  133.0 3.2 fusion.42
  136.3 0.9 copy.107
  137.1 9.1 all-to-all-start
  147.7 11.0 all-to-all-done
  160.8 110.7 %all-gather.12.cloned.1.call-done = bf16[2,384,3072]{2,0,1:T(2,128)(2,1)} async-done(((bf16[2,3,3072]{2,0,1:T(2,128)(2,1)}), bf16[2,384,3072]{2,0,1:T(2,128)(2,1)}) %all-gather.12.cloned.1.call-update) | async-done | bytes 4718608 | tf_op jit(solution)/shard_map/all_gather | solution.py:39
  271.5 10.8 fusion.119
  282.3 10.0 copy.110
  292.9 10.0 copy.112
  303.1 2.6 fusion.47
  306.6 114.2 %all-gather.14.cloned.1.call-done = bf16[1,384,3072]{2,0,1:T(2,128)(2,1)} async-done(((bf16[1,3,3072]{2,0,1:T(2,128)(2,1)}), bf16[1,384,3072]{2,0,1:T(2,128)(2,1)}) %all-gather.14.cloned.1.call-update) | async-done | bytes 2359312 | tf_op jit(solution)/shard_map/all_gather | solution.py:65
  420.7 3.1 fusion.63
  424.0 21.4 %all_to_all.81 = bf16[1,384,24]{2,0,1:T(2,128)(2,1)S(1)} all-to-all(bf16[1,384,24]{2,0,1:T(2,128)(2,1)S(1)} %copy.115), channel_id=1, replica_groups=mesh['section'=2,'blk'=128] {'blk'}, dimensions={1} | all-to-all | bytes 36864 | tf_op jit(solution)/shard_map/all_to_all | solution.py:69
  445.9 1.3 collective-permute-start
  447.2 0.8 collective-permute-done
  449.2 111.1 %all-gather.16.cloned.1.call-done = bf16[1,384,3072]{2,0,1:T(2,128)(2,1)} async-done(((bf16[1,3,3072]{2,0,1:T(2,128)(2,1)}), bf16[1,384,3072]{2,0,1:T(2,128)(2,1)}) %all-gather.16.cloned.1.call-update) | async-done | bytes 2359312 | tf_op jit(solution)/shard_map/all_gather | solution.py:21
  560.4 3.2 fusion.39
  563.6 0.8 copy.117
  564.5 9.1 all-to-all-start.2
  574.2 11.9 all-to-all-done.2
  588.1 110.7 %all-gather.18.cloned.1.call-done = bf16[2,384,3072]{2,0,1:T(2,128)(2,1)} async-done(((bf16[2,3,3072]{2,0,1:T(2,128)(2,1)}), bf16[2,384,3072]{2,0,1:T(2,128)(2,1)}) %all-gather.18.cloned.1.call-update) | async-done | bytes 4718608 | tf_op jit(solution)/shard_map/all_gather | solution.py:39
  698.8 10.8 fusion.118
  709.7 10.0 copy.120
  720.2 10.0 copy.122
  730.5 2.6 fusion.46
  733.9 114.2 %all-gather.20.cloned.1.call-done = bf16[1,384,3072]{2,0,1:T(2,128)(2,1)} async-done(((bf16[1,3,3072]{2,0,1:T(2,128)(2,1)}), bf16[1,384,3072]{2,0,1:T(2,128)(2,1)}) %all-gather.20.cloned.1.call-update) | async-done | bytes 2359312 | tf_op jit(solution)/shard_map/all_gather | solution.py:65
  848.1 3.1 fusion.60
  851.4 21.4 %all_to_all.82 = bf16[1,384,24]{2,0,1:T(2,128)(2,1)S(1)} all-to-all(bf16[1,384,24]{2,0,1:T(2,128)(2,1)S(1)} %copy.125), channel_id=1, replica_groups=mesh['section'=2,'blk'=128] {'blk'}, dimensions={1} | all-to-all | bytes 36864 | tf_op jit(solution)/shard_map/all_to_all | solution.py:69
  873.2 1.3 collective-permute-start.1
  874.5 0.8 collective-permute-done.1
  876.5 111.1 %all-gather.22.cloned.1.call-done = bf16[1,384,3072]{2,0,1:T(2,128)(2,1)} async-done(((bf16[1,3,3072]{2,0,1:T(2,128)(2,1)}), bf16[1,384,3072]{2,0,1:T(2,128)(2,1)}) %all-gather.22.cloned.1.call-update) | async-done | bytes 2359312 | tf_op jit(solution)/shard_map/all_gather | solution.py:21
  987.6 3.2 fusion.36
  990.9 0.8 copy.127
  991.7 9.1 all-to-all-start.4
  1001.5 11.8 all-to-all-done.4
  1015.4 110.7 %all-gather.24.cloned.1.call-done = bf16[2,384,3072]{2,0,1:T(2,128)(2,1)} async-done(((bf16[2,3,3072]{2,0,1:T(2,128)(2,1)}), bf16[2,384,3072]{2,0,1:T(2,128)(2,1)}) %all-gather.24.cloned.1.call-update) | async-done | bytes 4718608 | tf_op jit(solution)/shard_map/all_gather | solution.py:39
  1126.1 10.8 fusion.117
  1136.9 10.0 copy.130
  1147.5 10.0 copy.132
  1157.7 2.6 fusion.45
  1161.1 114.2 %all-gather.26.cloned.1.call-done = bf16[1,384,3072]{2,0,1:T(2,128)(2,1)} async-done(((bf16[1,3,3072]{2,0,1:T(2,128)(2,1)}), bf16[1,384,3072]{2,0,1:T(2,128)(2,1)}) %all-gather.26.cloned.1.call-update) | async-done | bytes 2359312 | tf_op jit(solution)/shard_map/all_gather | solution.py:65
  1275.3 3.1 fusion.57
  1278.4 0.9 copy.135
  1279.3 9.1 all-to-all-start.5
  1288.4 12.5 all-to-all-done.5
  (116 shorter events, 17.6 us)
Async XLA Ops:
  6.5 126.5 %copy-start = (bf16[1,3072,72]{1,2,0:T(8,128)(2,1)S(1)}, bf16[1,3072,72]{1,2,0:T(8,128)(2,1)}, u32[]{:S(2)}) copy-start(bf16[1,3072,72]{1,2,0:T(8,128)(2,1)} %param.10) | copy-start | bytes 1327108
  6.5 5.1 copy-start.1
  6.5 6.0 copy-start.3
  6.5 6.0 copy-start.2
  6.5 126.5 %all-gather.10.cloned.1.call-start = ((), (), s32[]{:S(2)}) async-start(), calls=%async_computation.6 | async-start | bytes 4755456 | tf_op jit(solution)/shard_map/all_gather | solution.py:21
  12.5 133.8 %copy-start.4 = (s32[1,2,128]{2,1,0:T(2,128)S(1)}, s32[1,2,128]{2,1,0:T(2,128)}, u32[]{:S(2)}) copy-start(s32[1,2,128]{2,1,0:T(2,128)} %param.14) | copy-start | bytes 3076
  12.8 147.7 %copy-start.6 = (s32[2,128]{1,0:T(2,128)S(1)}, s32[2,128]{1,0:T(2,128)}, u32[]{:S(2)}) copy-start(s32[2,128]{1,0:T(2,128)} %param.15) | copy-start | bytes 3076
  137.1 21.6 %all-to-all-start = ((bf16[1,384,72]{2,0,1:T(2,128)(2,1)}), bf16[1,384,72]{2,0,1:T(2,128)(2,1)S(1)}, u32[]{:S(2)}, u32[]{:S(2)}) async-start(bf16[1,384,72]{2,0,1:T(2,128)(2,1)} %copy.107), calls=%async_computation | async-start | bytes 393216 | tf_op jit(solution)/shard_map/all_to_all | solution.py:25
  146.2 125.3 %all-gather.12.cloned.1.call-start = ((), (), s32[]{:S(2)}) async-start(), calls=%async_computation.7 | async-start | bytes 4755456 | tf_op jit(solution)/shard_map/all_gather | solution.py:39
  160.4 260.4 %all-gather.14.cloned.1.call-start = ((), (), s32[]{:S(2)}) async-start(), calls=%async_computation.8 | async-start | bytes 4755456 | tf_op jit(solution)/shard_map/all_gather | solution.py:65
  302.9 117.9 %copy-start.5 = (bf16[1,3072,24]{1,2,0:T(8,128)(2,1)S(1)}, bf16[1,3072,24]{1,2,0:T(8,128)(2,1)}, u32[]{:S(2)}) copy-start(bf16[1,3072,24]{1,2,0:T(8,128)(2,1)} %param.11) | copy-start | bytes 442372
  306.5 253.9 %all-gather.16.cloned.1.call-start = ((), (), s32[]{:S(2)}) async-start(), calls=%async_computation.9 | async-start | bytes 4755456 | tf_op jit(solution)/shard_map/all_gather | solution.py:21
  445.9 2.1 collective-permute-start
  564.5 21.6 %all-to-all-start.2 = ((bf16[1,384,72]{2,0,1:T(2,128)(2,1)}), bf16[1,384,72]{2,0,1:T(2,128)(2,1)S(1)}, u32[]{:S(2)}, u32[]{:S(2)}) async-start(bf16[1,384,72]{2,0,1:T(2,128)(2,1)} %copy.117), calls=%async_computation.2 | async-start | bytes 393216 | tf_op jit(solution)/shard_map/all_to_all | solution.py:25
  573.5 125.3 %all-gather.18.cloned.1.call-start = ((), (), s32[]{:S(2)}) async-start(), calls=%async_computation.10 | async-start | bytes 4755456 | tf_op jit(solution)/shard_map/all_gather | solution.py:39
  587.7 260.3 %all-gather.20.cloned.1.call-start = ((), (), s32[]{:S(2)}) async-start(), calls=%async_computation.11 | async-start | bytes 4755456 | tf_op jit(solution)/shard_map/all_gather | solution.py:65
  733.8 253.8 %all-gather.22.cloned.1.call-start = ((), (), s32[]{:S(2)}) async-start(), calls=%async_computation.12 | async-start | bytes 4755456 | tf_op jit(solution)/shard_map/all_gather | solution.py:21
  873.2 2.1 collective-permute-start.1
  991.7 21.6 %all-to-all-start.4 = ((bf16[1,384,72]{2,0,1:T(2,128)(2,1)}), bf16[1,384,72]{2,0,1:T(2,128)(2,1)S(1)}, u32[]{:S(2)}, u32[]{:S(2)}) async-start(bf16[1,384,72]{2,0,1:T(2,128)(2,1)} %copy.127), calls=%async_computation.4 | async-start | bytes 393216 | tf_op jit(solution)/shard_map/all_to_all | solution.py:25
  1000.8 125.3 %all-gather.24.cloned.1.call-start = ((), (), s32[]{:S(2)}) async-start(), calls=%async_computation.13 | async-start | bytes 4755456 | tf_op jit(solution)/shard_map/all_gather | solution.py:39
  1015.0 260.3 %all-gather.26.cloned.1.call-start = ((), (), s32[]{:S(2)}) async-start(), calls=%async_computation.14 | async-start | bytes 4755456 | tf_op jit(solution)/shard_map/all_gather | solution.py:65
  1279.3 21.6 %all-to-all-start.5 = ((bf16[1,384,24]{2,0,1:T(2,128)(2,1)}), bf16[1,384,24]{2,0,1:T(2,128)(2,1)S(1)}, u32[]{:S(2)}, u32[]{:S(2)}) async-start(bf16[1,384,24]{2,0,1:T(2,128)(2,1)} %copy.135), calls=%async_computation.5 | async-start | bytes 393216 | tf_op jit(solution)/shard_map/all_to_all | solution.py:69
Sparse Core Ops, SparseCore 0:
  12.6 120.4 all-gather.9
  160.5 110.9 all-gather.11
  306.6 114.0 all-gather.13
  449.4 110.9 all-gather.15
  587.8 110.9 all-gather.17
  733.9 114.0 all-gather.19
  876.6 110.9 all-gather.21
  1015.1 110.9 all-gather.23
  1161.2 114.0 all-gather.25
